TPU v7x, 256 devices: a whole 4x4x8 slice. The times are simulated.
256 devices in a mesh: inp: 4 (over y_hi, core), dep: 8 (over x, y_lo), out: 8 (over z).
Axes of the slice: x: 4, y: 4 (y_hi: 2, y_lo: 2; y = y_hi * 2 + y_lo), z: 8, core: 2. Of those that a mesh axis runs over, the one named last changes fastest.
Arguments:
- tokens: bfloat16 [1024, 16384], P('inp', 'out'), may hold values from -6 to 6
- gate_up_weight: bfloat16 [16384, 2, 28672], P('out', None, ('inp', 'dep')), may hold values from -0.046875 to 0.046875
- down_weight: bfloat16 [28672, 16384], P(('inp', 'dep'), 'out'), may hold values from -0.03125 to 0.03125
Outputs:
- layer_output: bfloat16 [1024, 16384], P(('inp', 'dep'), 'out')
All inputs are finite; a program needn't handle non-finite values.
Results may differ from a plain program's by a relative error of at most 0.0049.
Values may be sent and summed in bfloat16 or wider, within the bound.
A program may use at most 128 MiB of HBM per device.

v0:
```python
import jax
import jax.numpy as jnp
from jax import lax
from jax.sharding import PartitionSpec as P


def swiglu(projected):
    return (jax.nn.silu(projected[:, 0, :]) * projected[:, 1, :]).astype(jnp.bfloat16)


def shards(tokens, gate_up_weight, down_weight):
    local_width = gate_up_weight.shape[0]
    block_units = gate_up_weight.shape[2]
    flat_weight = gate_up_weight.reshape(local_width, 2 * block_units)
    projected = jnp.dot(
        lax.all_gather(tokens, "inp", axis=0, tiled=True),
        flat_weight,
        preferred_element_type=jnp.float32,
    )
    projected = projected.reshape(projected.shape[0], 2, block_units)
    totals = lax.psum(projected, "out")
    full_hidden = swiglu(totals)
    result = lax.psum_scatter(
        jnp.dot(full_hidden, down_weight, preferred_element_type=jnp.float32),
        ("inp", "dep"),
        scatter_dimension=0,
        tiled=True,
    )
    return result.astype(jnp.bfloat16)


def solution(mesh):
    placed = (P("inp", "out"), P("out", None, ("inp", "dep")), P(("inp", "dep"), "out"))
    return jax.shard_map(
        shards, mesh=mesh, in_specs=placed, out_specs=P(("inp", "dep"), "out"), check_vma=False
    )
```

profile of v0, /device:TPU:10, one launch (start us, length us, event | category | flops | bytes accessed | tf_op | source)
XLA Modules:
  0.0 443.8 jit_solution(10383628695858579418)
XLA Ops:
  6.5 0.0 all-gather.2.cloned.1.call-start
  6.5 0.7 all-gather.2.cloned.1.call-update
  7.3 0.0 all-reduce.2.cloned.1.call-start
  7.3 7.6 %copy.5 = bf16[256,8,2,896]{3,1,2,0:T(8,128)(2,1)} copy(bf16[256,8,2,896]{3,2,1,0:T(2,128)(2,1)} %bitcast.23) | data formatting | bytes 14680064
  14.9 10.5 %copy.4 = bf16[1792,2048]{1,0:T(8,128)(2,1)} copy(bf16[1792,2048]{0,1:T(8,128)(2,1)} %bitcast.22) | data formatting | bytes 14680064 | tf_op jit(solution)/shard_map/dot_general | solution.py:15
  25.4 26.8 %all-gather.2.cloned.1.call-done = bf16[1024,2048]{1,0:T(8,128)(2,1)} async-done(((bf16[256,2048]{1,0:T(8,128)(2,1)}), bf16[1024,2048]{1,0:T(8,128)(2,1)}) %all-gather.2.cloned.1.call-update) | async-done | bytes 4194320 | tf_op jit(solution)/shard_map/all_gather | solution.py:16
  52.3 14.3 %fusion = f32[1024,2,896]{2,0,1:T(8,128)} fusion(bf16[2,896,2048]{2,1,0:T(8,128)(2,1)} %bitcast.24, bf16[1024,2048]{1,0:T(8,128)(2,1)} %all-gather.2.cloned.1.call-done), kind=kOutput, calls=%fused_computation | convolution fusion | flops 7516192768 | bytes 18874368 | tf_op jit(solution)/shard_map/dot_general | solution.py:15
  66.5 0.0 all-reduce.2.cloned.1.call-update
  66.6 0.0 reduce-scatter.2.cloned.1.call-start
  66.6 168.7 %all-reduce.2.cloned.1.call-done = f32[1024,2,896]{2,0,1:T(8,128)} async-done(((f32[1024,2,896]{2,0,1:T(8,128)}), f32[1024,2,896]{2,0,1:T(8,128)}) %all-reduce.2.cloned.1.call-update) | async-done | bytes 7340048 | tf_op jit(solution)/shard_map/psum | solution.py:21
  235.3 11.9 %fusion.4 = f32[1024,2048]{1,0:T(8,128)} fusion(bf16[896,2048]{1,0:T(8,128)(2,1)} %param.5, f32[1024,2,896]{2,0,1:T(8,128)} %all-reduce.2.cloned.1.call-done), kind=kOutput, calls=%fused_computation.6 | convolution fusion | flops 3763601408 | bytes 19398656 | tf_op jit(solution)/shard_map/dot_general | solution.py:24
  247.3 0.0 reduce-scatter.2.cloned.1.call-update
  247.3 188.3 %reduce-scatter.2.cloned.1.call-done = f32[32,2048]{1,0:T(8,128)} async-done(((f32[1024,2048]{1,0:T(8,128)}), f32[32,2048]{1,0:T(8,128)}) %reduce-scatter.2.cloned.1.call-update) | async-done | bytes 262160 | tf_op jit(solution)/shard_map/reduce_scatter | solution.py:23
  435.6 1.6 convert_element_type.7
Async XLA Ops:
  6.5 45.7 %all-gather.2.cloned.1.call-start = ((), (), s32[]{:S(2)}) async-start(), calls=%async_computation.1 | async-start | bytes 5242880 | tf_op jit(solution)/shard_map/all_gather | solution.py:16
  7.3 228.1 %all-reduce.2.cloned.1.call-start = ((), (), s32[]{:S(2)}) async-start(), calls=%async_computation.2 | async-start | bytes 14680064 | tf_op jit(solution)/shard_map/psum | solution.py:21
  66.6 369.1 %reduce-scatter.2.cloned.1.call-start = ((), (), s32[]{:S(2)}) async-start(), calls=%async_computation.3 | async-start | bytes 8650752 | tf_op jit(solution)/shard_map/reduce_scatter | solution.py:23
Sparse Core Ops, SparseCore 0:
  9.2 43.0 all-gather.1
  66.7 168.5 all-reduce.1
  247.4 188.1 reduce-scatter.1
where the time goes:
time: 444 us
  waiting for transfers between devices  385 us (87%)
  matrix products  26.2 us (6%)
  local copies, waits for them, and re-layouts  18.1 us (4%)
  between operations  13.1 us (3%)
    reduce_scatter x1, waiting for transfers between devices, shards(): lax.psum_scatter(jnp.dot(full_hidden, down_weight, preferred_element_type...  188 us
    psum x1, waiting for transfers between devices, shards(): totals = lax.psum(projected, 'out')  169 us
    all_gather x1, waiting for transfers between devices, shards(): lax.all_gather(tokens, 'inp', axis=0, tiled=True)  26.8 us
    dot_general x1, matrix products, shards(): jnp.dot(lax.all_gather(tokens, 'inp', axis=0, tiled=True), flat_weight, p...  14.3 us
    dot_general x1, matrix products, shards(): jnp.dot(full_hidden, down_weight, preferred_element_type=jnp.float32)  11.9 us
    dot_general x1, local copies, waits for them, and re-layouts, shards(): jnp.dot(lax.all_gather(tokens, 'inp', axis=0, tiled=True), flat_weight, p...  10.5 us
  transfers between devices with their start and end apart: 3, of which 3 were waited for; matrix products, arithmetic and copies ran while one was open for 4% of the time, Pallas kernels for 0%

commit v1 on v0

--- a/solution.py
+++ b/solution.py
@@ -18,7 +18,9 @@
         preferred_element_type=jnp.float32,
     )
     projected = projected.reshape(projected.shape[0], 2, block_units)
-    totals = lax.psum(projected, "out")
+    totals = projected
+    for hop in (1, 2, 4):
+        totals = totals + lax.ppermute(totals, "out", [(dev, dev ^ hop) for dev in range(8)])
     full_hidden = swiglu(totals)
     result = lax.psum_scatter(
         jnp.dot(full_hidden, down_weight, preferred_element_type=jnp.float32),

time: 444 us -> 1090 us (2.45)
  waiting for transfers between devices: 385 us -> 1000 us
  other arithmetic: 1.62 us -> 21.1 us
    ppermute x0 -> x3, waiting for transfers between devices: none -> 789 us  [shards(): lax.ppermute(totals, 'out', [(dev, dev ^ hop) for dev in range(8)])]
    psum x1 -> x0, waiting for transfers between devices: 169 us -> none  [shards(): totals = lax.psum(projected, 'out')]
    add x0 -> x3, other arithmetic: none -> 19.5 us  [shards(): totals + lax.ppermute(totals, 'out', [(dev, dev ^ hop) for dev in range(8)])]
  transfers between devices with their start and end apart: 3 -> 5, of which waited for: 3 -> 5; matrix products, arithmetic and copies ran while one was open for 4% -> 2% of each run, Pallas kernels for 0% -> 0%
where the time goes in v1:
time: 1090 us
  waiting for transfers between devices  1000 us (92%)
  matrix products  22.3 us (2%)
  other arithmetic  21.1 us (2%)
  local copies, waits for them, and re-layouts  19.5 us (2%)
  between operations  13.4 us (1%)
    ppermute x3, waiting for transfers between devices, shards(): lax.ppermute(totals, 'out', [(dev, dev ^ hop) for dev in range(8)])  789 us
    reduce_scatter x1, waiting for transfers between devices, shards(): lax.psum_scatter(jnp.dot(full_hidden, down_weight, preferred_element_type...  188 us
    all_gather x1, waiting for transfers between devices, shards(): lax.all_gather(tokens, 'inp', axis=0, tiled=True)  26.8 us
  transfers between devices with their start and end apart: 5, of which 5 were waited for; matrix products, arithmetic and copies ran while one was open for 2% of the time, Pallas kernels for 0%

profile of v1, /device:TPU:10, one launch (start us, length us, event | category | flops | bytes accessed | tf_op | source)
XLA Modules:
  0.0 1091.1 jit_solution(14033884754906178676)
XLA Ops:
  6.5 0.0 all-gather.2.cloned.1.call-start
  6.5 0.7 all-gather.2.cloned.1.call-update
  7.3 0.0 reduce-scatter.2.cloned.1.call-start
  7.3 7.6 copy.5
  14.9 10.6 copy.4
  25.5 26.8 %all-gather.2.cloned.1.call-done = bf16[1024,2048]{1,0:T(8,128)(2,1)} async-done(((bf16[256,2048]{1,0:T(8,128)(2,1)}), bf16[1024,2048]{1,0:T(8,128)(2,1)}) %all-gather.2.cloned.1.call-update) | async-done | bytes 4194320 | tf_op jit(solution)/shard_map/all_gather | solution.py:16
  52.3 12.4 %fusion = f32[1024,2,896]{2,0,1:T(8,128)S(1)} fusion(bf16[2,896,2048]{2,1,0:T(8,128)(2,1)} %bitcast.24, bf16[1024,2048]{1,0:T(8,128)(2,1)} %all-gather.2.cloned.1.call-done), kind=kOutput, calls=%fused_computation | convolution fusion | flops 7516192768 | bytes 18874368 | tf_op jit(solution)/shard_map/dot_general | solution.py:15
  64.7 0.0 copy-start
  64.7 1.6 collective-permute-start
  66.3 1.3 copy-done
  67.6 157.4 %collective-permute-done = f32[1024,2,896]{2,0,1:T(8,128)} collective-permute-done((f32[1024,2,896]{2,0,1:T(8,128)S(1)}, f32[1024,2,896]{2,0,1:T(8,128)}, u32[]{:S(2)}, u32[]{:S(2)}) %collective-permute-start) | collective-permute-done | bytes 7340064 | tf_op jit(solution)/shard_map/ppermute | solution.py:23
  225.0 5.9 add.15
  230.9 2.6 collective-permute-start.1
  233.5 315.1 %collective-permute-done.1 = f32[1024,2,896]{2,0,1:T(8,128)} collective-permute-done((f32[1024,2,896]{2,0,1:T(8,128)S(1)}, f32[1024,2,896]{2,0,1:T(8,128)}, u32[]{:S(2)}, u32[]{:S(2)}) %collective-permute-start.1) | collective-permute-done | bytes 7340064 | tf_op jit(solution)/shard_map/ppermute | solution.py:23
  548.6 6.8 add.16
  555.4 0.0 copy-start.1
  555.4 5.7 collective-permute-start.2
  561.1 316.9 %collective-permute-done.2 = f32[1024,2,896]{2,0,1:T(8,128)S(1)} collective-permute-done((f32[1024,2,896]{2,0,1:T(8,128)}, f32[1024,2,896]{2,0,1:T(8,128)S(1)}, u32[]{:S(2)}, u32[]{:S(2)}) %collective-permute-start.2) | collective-permute-done | bytes 7340064 | tf_op jit(solution)/shard_map/ppermute | solution.py:23
  878.0 6.8 add.17
  884.8 0.0 copy-done.1
  884.8 9.9 fusion.4
  894.8 0.0 reduce-scatter.2.cloned.1.call-update
  894.8 187.9 %reduce-scatter.2.cloned.1.call-done = f32[32,2048]{1,0:T(8,128)} async-done(((f32[1024,2048]{1,0:T(8,128)}), f32[32,2048]{1,0:T(8,128)}) %reduce-scatter.2.cloned.1.call-update) | async-done | bytes 262160 | tf_op jit(solution)/shard_map/reduce_scatter | solution.py:25
  1082.6 1.6 convert_element_type.7
Async XLA Ops:
  6.5 45.7 %all-gather.2.cloned.1.call-start = ((), (), s32[]{:S(2)}) async-start(), calls=%async_computation.1 | async-start | bytes 5242880 | tf_op jit(solution)/shard_map/all_gather | solution.py:16
  7.3 1075.4 %reduce-scatter.2.cloned.1.call-start = ((), (), s32[]{:S(2)}) async-start(), calls=%async_computation.2 | async-start | bytes 8650752 | tf_op jit(solution)/shard_map/reduce_scatter | solution.py:25
  64.7 2.9 copy-start
  64.7 160.3 %collective-permute-start = (f32[1024,2,896]{2,0,1:T(8,128)S(1)}, f32[1024,2,896]{2,0,1:T(8,128)}, u32[]{:S(2)}, u32[]{:S(2)}) collective-permute-start(f32[1024,2,896]{2,0,1:T(8,128)S(1)} %fusion), channel_id=1, source_target_pairs={{0,1},{1,0},{2,3},{3,2},{4,5},{5,4},{6,7},{7,6},{8,9},{9,8},{10,11... | collective-permute-start | bytes 22020104 | tf_op jit(solution)/shard_map/ppermute | solution.py:23
  230.9 317.7 %collective-permute-start.1 = (f32[1024,2,896]{2,0,1:T(8,128)S(1)}, f32[1024,2,896]{2,0,1:T(8,128)}, u32[]{:S(2)}, u32[]{:S(2)}) collective-permute-start(f32[1024,2,896]{2,0,1:T(8,128)S(1)} %add.15), channel_id=1, source_target_pairs={{0,2},{1,3},{2,0},{3,1},{4,6},{5,7},{6,4},{7,5},{8,10},{9,11},{10,... | collective-permute-start | bytes 22020104 | tf_op jit(solution)/shard_map/ppermute | solution.py:23
  555.4 329.4 %copy-start.1 = (bf16[896,2048]{1,0:T(8,128)(2,1)S(1)}, bf16[896,2048]{1,0:T(8,128)(2,1)}, u32[]{:S(2)}) copy-start(bf16[896,2048]{1,0:T(8,128)(2,1)} %param.5) | copy-start | bytes 11010052
  555.4 322.6 %collective-permute-start.2 = (f32[1024,2,896]{2,0,1:T(8,128)}, f32[1024,2,896]{2,0,1:T(8,128)S(1)}, u32[]{:S(2)}, u32[]{:S(2)}) collective-permute-start(f32[1024,2,896]{2,0,1:T(8,128)} %add.16), channel_id=1, source_target_pairs={{0,4},{1,5},{2,6},{3,7},{4,0},{5,1},{6,2},{7,3},{8,12},{9,13},{10,... | collective-permute-start | bytes 22020104 | tf_op jit(solution)/shard_map/ppermute | solution.py:23
Sparse Core Ops, SparseCore 0:
  9.2 43.0 all-gather.1
  894.9 187.6 reduce-scatter.1

commit v2 on v0

--- a/solution.py
+++ b/solution.py
@@ -13,7 +13,9 @@
     block_units = gate_up_weight.shape[2]
     flat_weight = gate_up_weight.reshape(local_width, 2 * block_units)
     projected = jnp.dot(
-        lax.all_gather(tokens, "inp", axis=0, tiled=True),
+        jnp.concatenate(
+            lax.all_to_all(jnp.stack([tokens] * lax.axis_size("inp")), "inp", 0, 0), axis=0
+        ),
         flat_weight,
         preferred_element_type=jnp.float32,
     )

time: 444 us -> 458 us (1.032)
  starting transfers between devices: 0.08 us -> 4.95 us
    all_to_all x0 -> x1, waiting for transfers between devices: none -> 31.5 us  [shards(): lax.all_to_all(jnp.stack([tokens] * lax.axis_size('inp')), 'inp', 0, 0)]
    all_gather x1 -> x0, waiting for transfers between devices: 26.8 us -> none  [shards(): lax.all_gather(tokens, 'inp', axis=0, tiled=True)]
    all_to_all x0 -> x1, starting transfers between devices: none -> 4.87 us  [shards(): lax.all_to_all(jnp.stack([tokens] * lax.axis_size('inp')), 'inp', 0, 0)]
where the time goes in v2:
time: 458 us
  waiting for transfers between devices  389 us (85%)
  matrix products  26.2 us (6%)
  local copies, waits for them, and re-layouts  21.9 us (5%)
  between operations  13.4 us (3%)
  starting transfers between devices  4.95 us (1%)
    reduce_scatter x1, waiting for transfers between devices, shards(): lax.psum_scatter(jnp.dot(full_hidden, down_weight, preferred_element_type...  188 us
    psum x1, waiting for transfers between devices, shards(): totals = lax.psum(projected, 'out')  170 us
    all_to_all x1, waiting for transfers between devices, shards(): lax.all_to_all(jnp.stack([tokens] * lax.axis_size('inp')), 'inp', 0, 0)  31.5 us
    dot_general x1, matrix products, shards(): jnp.dot(jnp.concatenate(lax.all_to_all(jnp.stack([tokens] * lax.axis_size...  14.3 us
    dot_general x1, matrix products, shards(): jnp.dot(full_hidden, down_weight, preferred_element_type=jnp.float32)  11.9 us
    dot_general x1, local copies, waits for them, and re-layouts, shards(): jnp.dot(jnp.concatenate(lax.all_to_all(jnp.stack([tokens] * lax.axis_size...  10.5 us
  transfers between devices with their start and end apart: 3, of which 3 were waited for; matrix products, arithmetic and copies ran while one was open for 4% of the time, Pallas kernels for 0%

profile of v2, /device:TPU:10, one launch (start us, length us, event | category | flops | bytes accessed | tf_op | source)
XLA Modules:
  0.0 457.6 jit_solution(18367404070961263274)
XLA Ops:
  6.5 3.8 stack.2
  10.3 4.9 %all-to-all-start = ((bf16[4,256,2048]{2,1,0:T(8,128)(2,1)}), bf16[4,256,2048]{2,1,0:T(8,128)(2,1)}, u32[]{:S(2)}, u32[]{:S(2)}) async-start(bf16[4,256,2048]{2,1,0:T(8,128)(2,1)} %stack.2), calls=%async_computation | async-start | bytes 8388608 | tf_op jit(solution)/shard_map/all_to_all | solution.py:17
  15.2 0.0 all-reduce.2.cloned.1.call-start
  15.2 7.6 %copy.5 = bf16[256,8,2,896]{3,1,2,0:T(8,128)(2,1)} copy(bf16[256,8,2,896]{3,2,1,0:T(2,128)(2,1)} %bitcast.24) | data formatting | bytes 14680064
  22.8 10.5 %copy.4 = bf16[1792,2048]{1,0:T(8,128)(2,1)} copy(bf16[1792,2048]{0,1:T(8,128)(2,1)} %bitcast.23) | data formatting | bytes 14680064 | tf_op jit(solution)/shard_map/dot_general | solution.py:15
  33.4 31.5 %all-to-all-done = bf16[4,256,2048]{2,1,0:T(8,128)(2,1)} async-done(((bf16[4,256,2048]{2,1,0:T(8,128)(2,1)}), bf16[4,256,2048]{2,1,0:T(8,128)(2,1)}, u32[]{:S(2)}, u32[]{:S(2)}) %all-to-all-start) | async-done | bytes 4194336 | tf_op jit(solution)/shard_map/all_to_all | solution.py:17
  64.9 14.3 %fusion.6 = f32[1024,2,896]{2,0,1:T(8,128)} fusion(bf16[1024,2048,1]{1,0,2:T(8,128)(2,1)} %bitcast.1, bf16[2,896,2048]{2,1,0:T(8,128)(2,1)} %bitcast.25), kind=kOutput, calls=%fused_computation.7 | convolution fusion | flops 7516192768 | bytes 18874368 | tf_op jit(solution)/shard_map/dot_general | solution.py:15
  79.2 0.0 all-reduce.2.cloned.1.call-update
  79.2 0.0 reduce-scatter.2.cloned.1.call-start
  79.3 169.6 %all-reduce.2.cloned.1.call-done = f32[1024,2,896]{2,0,1:T(8,128)} async-done(((f32[1024,2,896]{2,0,1:T(8,128)}), f32[1024,2,896]{2,0,1:T(8,128)}) %all-reduce.2.cloned.1.call-update) | async-done | bytes 7340048 | tf_op jit(solution)/shard_map/psum | solution.py:23
  248.9 11.9 %fusion.2 = f32[1024,2048]{1,0:T(8,128)} fusion(bf16[896,2048]{1,0:T(8,128)(2,1)} %param.5, f32[1024,2,896]{2,0,1:T(8,128)} %all-reduce.2.cloned.1.call-done), kind=kOutput, calls=%fused_computation.4 | convolution fusion | flops 3763601408 | bytes 19398656 | tf_op jit(solution)/shard_map/dot_general | solution.py:26
  260.8 0.0 reduce-scatter.2.cloned.1.call-update
  260.9 188.2 %reduce-scatter.2.cloned.1.call-done = f32[32,2048]{1,0:T(8,128)} async-done(((f32[1024,2048]{1,0:T(8,128)}), f32[32,2048]{1,0:T(8,128)}) %reduce-scatter.2.cloned.1.call-update) | async-done | bytes 262160 | tf_op jit(solution)/shard_map/reduce_scatter | solution.py:25
  449.1 1.6 convert_element_type.7
Async XLA Ops:
  10.3 54.6 %all-to-all-start = ((bf16[4,256,2048]{2,1,0:T(8,128)(2,1)}), bf16[4,256,2048]{2,1,0:T(8,128)(2,1)}, u32[]{:S(2)}, u32[]{:S(2)}) async-start(bf16[4,256,2048]{2,1,0:T(8,128)(2,1)} %stack.2), calls=%async_computation | async-start | bytes 8388608 | tf_op jit(solution)/shard_map/all_to_all | solution.py:17
  15.2 233.7 %all-reduce.2.cloned.1.call-start = ((), (), s32[]{:S(2)}) async-start(), calls=%async_computation.2 | async-start | bytes 14680064 | tf_op jit(solution)/shard_map/psum | solution.py:23
  79.2 369.9 %reduce-scatter.2.cloned.1.call-start = ((), (), s32[]{:S(2)}) async-start(), calls=%async_computation.3 | async-start | bytes 8650752 | tf_op jit(solution)/shard_map/reduce_scatter | solution.py:25
Sparse Core Ops, SparseCore 0:
  79.3 169.5 all-reduce.1
  261.0 188.0 reduce-scatter.1
